TPU v7x, 32 devices: a whole 2x2x4 slice. The times are simulated.
32 devices in a mesh: groups: 2 (over x), tower: 2 (over core), inner: 8 (over z, y).
Axes of the slice: x: 2, y: 2, z: 4, core: 2. Of those that a mesh axis runs over, the one named last changes fastest.
Arguments:
- ids: int32 [2, 64, 2048, 4], P('tower', 'inner', 'groups'), parts along dimension 2, may hold values from 0 to 16383
- bag_len: int32 [2, 64, 2048], P('tower', 'inner', 'groups'), parts along dimension 2, may hold values from 1 to 4
- slot_of_feature: int32 [2, 64], P('tower'), may hold values from 0 to 63, each once within a row
- tables: bfloat16 [2, 64, 16384, 24], P('tower', 'inner'), may hold values from -3 to 3
- cross_w: bfloat16 [2, 1536, 1536], P('tower'), may hold values from -0.15625 to 0.15625
- cross_b: float32 [2, 1536], P('tower'), may hold values from -3 to 3
- comp_w: bfloat16 [2, 1536, 64], P('tower'), may hold values from -0.15625 to 0.15625
- comp_b: float32 [2, 64], P('tower'), may hold values from -3 to 3
- other_towers: bfloat16 [2048, 896], P(('groups', 'inner')), parts along dimension 0, may hold values from -6 to 6
- expert_w: bfloat16 [8, 1024, 512], P('tower'), may hold values from -0.1875 to 0.1875
- expert_b: float32 [8, 512], P('tower'), may hold values from -3 to 3
- gate_w: bfloat16 [1024, 4, 8], replicated, may hold values from -0.1875 to 0.1875
Outputs:
- task_mix: bfloat16 [2048, 4, 512], P(('groups', 'inner'), None, 'tower'), parts along dimension 0
There are 2 independent parts, one for each index of `groups`. A program takes and returns all parts, laid end to end along the dimension named above; an argument that names none is the same for every part. Nothing has to cross between parts.
Inputs may be any that keep to these rules, and one draw needn't show every extreme that they name: `bag_len`: every bag holds at least one id. `slot_of_feature`: each row is a permutation of the 64 slots.
All inputs are finite; a program needn't handle non-finite values.
Results may differ from a plain program's by a relative error of at most 0.0095.
Values may be sent and summed in bfloat16 or wider, within the bound.
A program may use at most 128 MiB of HBM per device.

v0:
```python
import jax
import jax.numpy as jnp
from jax import lax
from jax.sharding import PartitionSpec as P


def pool_features(lookup, indices, lengths):
    feature_count = lookup.shape[0]
    vocab_rows = lookup.shape[1]
    embed_width = lookup.shape[2]
    sample_count = indices.shape[1]
    bag_size = indices.shape[2]
    offsets = (jnp.arange(feature_count) * vocab_rows)[:, None, None]
    flat_ids = (indices + offsets).reshape(feature_count * sample_count * bag_size)
    flat_table = lookup.reshape(feature_count * vocab_rows, embed_width)
    gathered = jnp.take(flat_table, flat_ids, axis=0, mode="clip")
    gathered = gathered.reshape(feature_count, sample_count, bag_size, embed_width)
    in_bag = (jnp.arange(bag_size)[None, None, :] < lengths[:, :, None]).astype(jnp.bfloat16)
    summed = jnp.einsum("fsbd,fsb->fsd", gathered, in_bag, preferred_element_type=jnp.float32)
    return summed.astype(jnp.bfloat16)


def on_device(
    ids,
    bag_len,
    slot_of_feature,
    tables,
    cross_w,
    cross_b,
    comp_w,
    comp_b,
    other_towers,
    expert_w,
    expert_b,
    gate_w,
):
    inner_size = lax.axis_size("inner")
    tower_size = lax.axis_size("tower")
    feature_count = tables.shape[1]
    sample_count = ids.shape[2]
    embed_width = tables.shape[3]
    pooled_all = pool_features(tables[0], ids[0], bag_len[0])
    pooled = jnp.transpose(pooled_all, (1, 0, 2)).reshape(sample_count, feature_count * embed_width)
    row_count = sample_count // inner_size
    block_rows = min(row_count, 128)
    block_count = row_count // block_rows
    sendable = pooled.reshape(inner_size, block_count, block_rows, feature_count * embed_width)
    slot_total = slot_of_feature.shape[1]
    onehot = (slot_of_feature[0][:, None] == jnp.arange(slot_total)[None, :]).astype(jnp.bfloat16)
    received = lax.all_to_all(sendable, "inner", split_axis=0, concat_axis=3, tiled=True)
    item_count = received.shape[1]
    full_width = received.shape[3]
    features = received.reshape(item_count * block_rows, slot_total, full_width // slot_total)
    first_layer = jnp.einsum("rfd,fg->rgd", features, onehot, preferred_element_type=jnp.float32)
    first_layer = first_layer.astype(jnp.bfloat16).reshape(item_count * block_rows, full_width)
    crossed = jnp.dot(first_layer, cross_w[0], preferred_element_type=jnp.float32) + cross_b[0]
    base = first_layer.astype(jnp.float32)
    next_layer = (base * crossed + base).astype(jnp.bfloat16)
    squeezed = jnp.dot(next_layer, comp_w[0], preferred_element_type=jnp.float32) + comp_b[0]
    compressed = squeezed.astype(jnp.bfloat16).reshape(item_count, block_rows, squeezed.shape[1])
    compressed = compressed.reshape(row_count, compressed.shape[2])
    gathered = lax.all_gather(compressed, "tower", axis=1, tiled=True)
    expert_in = jnp.concatenate([other_towers, gathered], axis=1)
    logits = jnp.einsum("ri,ike->rke", expert_in, gate_w, preferred_element_type=jnp.float32)
    weights = jnp.exp(logits)
    gate_probs = weights / jnp.sum(weights, axis=2, keepdims=True)
    hidden = jnp.einsum("ri,eih->erh", expert_in, expert_w, preferred_element_type=jnp.float32)
    hidden = jnp.maximum(hidden + expert_b[:, None, :], 0.0).astype(jnp.bfloat16)
    exp_local = expert_w.shape[0]
    task_count = gate_w.shape[1]
    hidden_width = hidden.shape[2]
    halves = hidden.reshape(exp_local, row_count, tower_size, hidden_width // tower_size)
    received_all = lax.all_to_all(halves, "tower", split_axis=2, concat_axis=0, tiled=True)
    running = jnp.zeros((row_count, task_count, hidden_width // tower_size), jnp.float32)
    for member in range(exp_local * tower_size):
        running = (
            running
            + gate_probs[:, :, member, None]
            * received_all[member, :, 0, :].astype(jnp.float32)[:, None, :]
        )
    task_mix = running.astype(jnp.bfloat16)
    return task_mix


def solution(mesh):
    return jax.shard_map(
        on_device,
        mesh=mesh,
        in_specs=(
            P("tower", "inner", "groups", None),
            P("tower", "inner", "groups"),
            P("tower", None),
            P("tower", "inner", None, None),
            P("tower", None, None),
            P("tower", None),
            P("tower", None, None),
            P("tower", None),
            P(("groups", "inner"), None),
            P("tower", None, None),
            P("tower", None),
            P(),
        ),
        out_specs=P(("groups", "inner"), None, "tower"),
        check_vma=False,
    )
```

profile of v0, /device:TPU:0, one launch (start us, length us, event | category | flops | bytes accessed | tf_op | source)
XLA Modules:
  0.0 630.7 jit_solution(350731891534048785)
XLA Ops:
  0.0 0.0 copy-start
  0.0 24.4 %copy.54 = bf16[1,8,16384,24]{3,2,1,0:T(8,128)(2,1)} copy(bf16[1,8,16384,24]{2,3,1,0:T(8,128)(2,1)} %param.15) | data formatting | bytes 12582912 | tf_op args[3]
  24.4 2.4 add.70
  26.8 6.1 add.71
  32.9 0.0 copy-done.2
  32.9 0.0 copy-start.3
  32.9 2.7 copy.55
  35.6 6.1 squeeze.6
  41.7 0.1 add.72
  41.9 0.0 copy-done.3
  41.9 2.6 copy.77
  44.6 501.1 %gather_fusion = bf16[32768,24]{1,0:T(8,128)(2,1)} fusion(bf16[131072,24]{1,0:T(8,128)(2,1)} %bitcast.123, s32[32768]{0:T(1024)S(1)} %broadcast_clamp_fusion), kind=kCustom, calls=%fused_computation | custom fusion | bytes 3276800 | tf_op jit(solution)/shard_map/jit(_take)/gather | solution.py:16
  545.7 46.9 %multiply_reduce_fusion = bf16[1024,8,24]{2,0,1:T(8,128)(2,1)S(1)} fusion(bf16[1024,8,4,24]{3,2,0,1:T(4,128)(2,1)} %bitcast.124, f32[1024,8,4]{2,0,1:T(8,128)} %copy.77), kind=kLoop, calls=%fused_computation.1 | loop fusion | flops 2162688 | bytes 2097152
  592.6 0.0 copy-start.5
  592.6 0.0 copy-start.7
  592.6 0.0 copy-start.6
  592.7 0.8 copy.76
  593.4 0.1 copy.79
  593.5 0.0 copy-start.1
  593.5 0.0 copy-start.8
  593.5 0.8 copy.56
  594.3 9.4 %all-to-all-start = ((bf16[8,1,128,192]{2,3,1,0:T(8,128)(2,1)}), bf16[8,1,128,192]{2,3,1,0:T(8,128)(2,1)S(1)}, u32[]{:S(2)}, u32[]{:S(2)}) async-start(bf16[8,1,128,192]{2,3,1,0:T(8,128)(2,1)} %copy.56), calls=%async_computation | async-start | bytes 786432 | tf_op jit(solution)/shard_map/all_to_all | solution.py:50
  603.7 0.0 copy-done.5
  603.7 0.0 copy-start.4
  603.7 10.2 %all-to-all-done = bf16[8,1,128,192]{2,3,1,0:T(8,128)(2,1)S(1)} async-done(((bf16[8,1,128,192]{2,3,1,0:T(8,128)(2,1)}), bf16[8,1,128,192]{2,3,1,0:T(8,128)(2,1)S(1)}, u32[]{:S(2)}, u32[]{:S(2)}) %all-to-all-start) | async-done | bytes 393248 | tf_op jit(solution)/shard_map/all_to_all | solution.py:50
  614.0 0.0 copy-done.7
  614.0 0.2 fusion.16
  614.2 0.3 copy.58
  614.5 0.2 copy.59
  614.7 0.0 copy-done
  614.7 0.0 copy-done.6
  614.7 3.3 fusion.23
  618.0 1.8 all_gather.3
  619.9 0.1 copy.60
  620.0 0.0 copy-done.1
  620.0 0.2 fusion.49
  620.2 0.1 copy.61
  620.4 0.1 copy.63
  620.5 0.1 copy.64
  620.6 0.1 copy.65
  620.7 0.1 copy.66
  620.8 0.1 copy.67
  620.9 0.1 copy.68
  621.0 0.1 copy.69
  621.2 2.9 fusion.15
  624.1 4.2 all_to_all.33
  628.3 0.1 fusion.41
  628.4 2.3 add_convert_fusion
  (10 shorter events, 0.1 us)
Async XLA Ops:
  0.0 614.7 %copy-start = (bf16[1,1536,64]{1,2,0:T(8,128)(2,1)S(1)}, bf16[1,1536,64]{1,2,0:T(8,128)(2,1)}, u32[]{:S(2)}) copy-start(bf16[1,1536,64]{1,2,0:T(8,128)(2,1)} %param.18) | copy-start | bytes 589828
  24.4 8.5 %copy-start.2 = (s32[1,8,1024,4]{2,3,1,0:T(4,128)S(1)}, s32[1,8,1024,4]{2,3,1,0:T(4,128)}, u32[]{:S(2)}) copy-start(s32[1,8,1024,4]{2,3,1,0:T(4,128)} %param.12) | copy-start | bytes 393220
  32.9 9.0 %copy-start.3 = (s32[1,8,1024]{2,1,0:T(8,128)S(1)}, s32[1,8,1024]{2,1,0:T(8,128)}, u32[]{:S(2)}) copy-start(s32[1,8,1024]{2,1,0:T(8,128)} %param.13) | copy-start | bytes 98308
  592.6 11.1 %copy-start.5 = (f32[1,1536]{1,0:T(1,128)S(1)}, f32[1,1536]{1,0:T(1,128)}, u32[]{:S(2)}) copy-start(f32[1,1536]{1,0:T(1,128)} %param.17) | copy-start | bytes 18436
  592.6 21.3 %copy-start.7 = (s32[1,64]{1,0:T(1,128)S(1)}, s32[1,64]{1,0:T(1,128)}, u32[]{:S(2)}) copy-start(s32[1,64]{1,0:T(1,128)} %param.14) | copy-start | bytes 772
  592.6 22.0 %copy-start.6 = (f32[1,64]{1,0:T(1,128)S(1)}, f32[1,64]{1,0:T(1,128)}, u32[]{:S(2)}) copy-start(f32[1,64]{1,0:T(1,128)} %param.19) | copy-start | bytes 772
  593.5 26.5 %copy-start.1 = (bf16[128,896]{1,0:T(8,128)(2,1)S(1)}, bf16[128,896]{1,0:T(8,128)(2,1)}, u32[]{:S(2)}) copy-start(bf16[128,896]{1,0:T(8,128)(2,1)} %param.20) | copy-start | bytes 688132
  593.5 26.5 %copy-start.8 = (bf16[1024,4,8]{0,2,1:T(8,128)(2,1)S(1)}, bf16[1024,4,8]{0,2,1:T(8,128)(2,1)}, u32[]{:S(2)}) copy-start(bf16[1024,4,8]{0,2,1:T(8,128)(2,1)} %param.23) | copy-start | bytes 196612
  594.3 19.6 %all-to-all-start = ((bf16[8,1,128,192]{2,3,1,0:T(8,128)(2,1)}), bf16[8,1,128,192]{2,3,1,0:T(8,128)(2,1)S(1)}, u32[]{:S(2)}, u32[]{:S(2)}) async-start(bf16[8,1,128,192]{2,3,1,0:T(8,128)(2,1)} %copy.56), calls=%async_computation | async-start | bytes 786432 | tf_op jit(solution)/shard_map/all_to_all | solution.py:50
  603.7 17.5 %copy-start.4 = (f32[4,512]{1,0:T(4,128)S(1)}, f32[4,512]{1,0:T(4,128)}, u32[]{:S(2)}) copy-start(f32[4,512]{1,0:T(4,128)} %param.22) | copy-start | bytes 24580
where the time goes:
time: 635 us; the launch traced here: 631 us
  local copies, waits for them, and re-layouts  549 us (86%)
  other arithmetic  49.6 us (8%)
  waiting for transfers between devices  10.2 us (2%)
  starting transfers between devices  9.35 us (1%)
  matrix products  6.7 us (1%)
    gather x1, local copies, waits for them, and re-layouts, pool_features(): gathered = jnp.take(flat_table, flat_ids, axis=0, mode='clip')  501 us
    unnamed x3, other arithmetic  47 us
    unnamed x22, local copies, waits for them, and re-layouts  29.8 us
  transfers between devices with their start and end apart: 1, of which 1 were waited for; matrix products, arithmetic and copies ran while one was open for 0% of the time, Pallas kernels for 0%

commit v1 on v0

v1 whole, which is shorter than its diff:
```python
import functools
import jax
import jax.numpy as jnp
from jax import lax
from jax.experimental import pallas as pl
from jax.experimental.pallas import tpu as pltpu
from jax.sharding import PartitionSpec as P

MESH = pl.DeviceIdType.MESH


def pool_kernel(bag, unroll, ids_ref, tab_ref, out_ref, rows_ref, acc_ref):
    group, width, vocab = tab_ref.shape
    dests, _, block = out_ref.shape
    samples = dests * block
    lanes = rows_ref.shape[1]
    first = pl.program_id(0) * (group * bag * samples)

    def turn(c, carry):
        at = pl.multiple_of(c * lanes, lanes)
        parts = [tab_ref[f, :, pl.ds(at, lanes)].astype(jnp.float32) for f in range(group)]
        if lanes > group * width:
            parts.append(jnp.zeros((lanes - group * width, lanes), jnp.float32))
        rows_ref[pl.ds(at, lanes), :] = jnp.concatenate(parts, axis=0).T
        return carry

    lax.fori_loop(0, vocab // lanes, turn, 0)
    rows_ref[pl.ds(vocab, 8), :] = jnp.zeros((8, lanes), jnp.float32)
    lane = lax.broadcasted_iota(jnp.int32, (1, lanes), 1)
    inside = [lane < (f + 1) * width for f in range(group)]

    def look(n, carry):
        base = n * unroll
        for u in range(unroll):
            total = None
            for f in reversed(range(group)):
                got = [
                    rows_ref[pl.ds(ids_ref[first + (f * bag + j) * samples + base + u], 1), :]
                    for j in range(bag)
                ]
                while len(got) > 1:
                    got = [a + b for a, b in zip(got[::2], got[1::2])] + got[len(got) & ~1 :]
                total = got[0] if total is None else jnp.where(inside[f], got[0], total)
            acc_ref[pl.ds(base + u, 1), :] = total
        return carry

    lax.fori_loop(0, samples // unroll, look, 0)
    for d in range(dests):
        turned = acc_ref[pl.ds(d * block, block), :].T
        out_ref[d] = turned[: group * width].astype(out_ref.dtype)


def pool(tables, ids, lengths, dests, unroll=16):
    features, vocab, width = tables.shape
    samples, bag = ids.shape[1:]
    group = max(g for g in range(1, features + 1) if features % g == 0 and g * width <= 128)
    in_bag = jnp.arange(bag)[None, :, None] < lengths[:, None, :]
    flat = jnp.where(in_bag, jnp.transpose(ids, (0, 2, 1)), vocab).reshape(-1)
    return pl.pallas_call(
        functools.partial(pool_kernel, bag, unroll),
        out_shape=jax.ShapeDtypeStruct((dests, features * width, samples // dests), jnp.bfloat16),
        grid_spec=pltpu.PrefetchScalarGridSpec(
            num_scalar_prefetch=1,
            grid=(features // group,),
            in_specs=[pl.BlockSpec((group, width, vocab), lambda i, ids: (i, 0, 0))],
            out_specs=pl.BlockSpec((dests, group * width, samples // dests), lambda i, ids: (0, i, 0)),
            scratch_shapes=[
                pltpu.VMEM((vocab + 8, 128), jnp.float32),
                pltpu.VMEM((samples, 128), jnp.float32),
            ],
        ),
        compiler_params=pltpu.CompilerParams(vmem_limit_bytes=48 * 2**20),
    )(flat, jnp.transpose(tables, (0, 2, 1)))


def dense_kernel(
    inverse_ref, send_ref, cross_w, cross_b_ref, comp_w_ref, comp_b_ref, other_ref, expert_w_hbm, expert_b_ref, gate_ref,
    out_ref,
    recv, stage, placed, first, expert_w, partial, squeezed, hidden_out, hidden_in,
    load_sem, own_sem, send_sem, recv_sem, comp_send, comp_recv, hid_send, hid_recv,
):
    inner, towers = lax.axis_size("inner"), lax.axis_size("tower")
    me, tower = lax.axis_index("inner"), lax.axis_index("tower")
    _, share, rows = recv.shape
    experts, expert_width, _ = expert_w.shape
    other_width = other_ref.shape[1]
    half = hidden_in.shape[3]
    slots = inverse_ref.shape[0]
    width = stage.shape[1]
    tasks = gate_ref.shape[0] // (experts * towers)

    load_experts = pltpu.make_async_copy(expert_w_hbm, expert_w, load_sem)
    load_experts.start()
    barrier = pltpu.get_barrier_semaphore()
    for off in range(1, inner):
        pl.semaphore_signal(barrier, inc=1, device_id={"inner": lax.rem(me + off, inner)}, device_id_type=MESH)
    for off in range(1, towers):
        pl.semaphore_signal(barrier, inc=1, device_id={"tower": lax.rem(tower + off, towers)}, device_id_type=MESH)
    pl.semaphore_wait(barrier, inner + towers - 2)

    blocks = []
    for off in range(1, inner):
        peer = lax.rem(me + off, inner)
        copy = pltpu.make_async_remote_copy(
            src_ref=send_ref.at[peer],
            dst_ref=recv.at[me],
            send_sem=send_sem.at[off],
            recv_sem=recv_sem.at[off],
            device_id={"inner": peer},
            device_id_type=MESH,
        )
        copy.start()
        blocks.append(copy)
    own = pltpu.make_async_copy(send_ref.at[me], recv.at[me], own_sem)
    own.start()

    other = other_ref[...]
    nt = (((1,), (1,)), ((), ()))
    logits = lax.dot_general(other, gate_ref[:, :other_width], nt, preferred_element_type=jnp.float32)
    load_experts.wait()
    for e in range(experts):
        partial[e] = (
            jnp.dot(other, expert_w[e, :other_width, :], preferred_element_type=jnp.float32) + expert_b_ref[e : e + 1, :]
        )
    own.wait()
    for copy in blocks:
        copy.wait()

    for i in range(inner):
        held = share // width
        stage[i * held : (i + 1) * held] = recv[i].astype(jnp.float32).reshape(held, width, rows)
    for g in range(slots):
        placed[g * width : (g + 1) * width, :] = stage[inverse_ref[g]]
    total = slots * width
    for c in range(0, total, 128):
        first[:, c : c + 128] = placed[c : c + 128, :].T
    base_low = first[...].astype(jnp.bfloat16)
    second = []
    step = 512 if total % 512 == 0 else 128
    for c in range(0, total, step):
        crossed = jnp.dot(base_low, cross_w[:, c : c + step], preferred_element_type=jnp.float32)
        crossed = crossed + cross_b_ref[:, c : c + step]
        base = first[:, c : c + step]
        second.append((base * crossed + base).astype(jnp.bfloat16))
    second = jnp.concatenate(second, axis=1)
    packed = lax.dot_general(second, comp_w_ref[...], nt, preferred_element_type=jnp.float32) + comp_b_ref[...]
    squeezed[tower] = packed.astype(jnp.bfloat16)
    shares = []
    for off in range(1, towers):
        copy = pltpu.make_async_remote_copy(
            src_ref=squeezed.at[tower],
            dst_ref=squeezed.at[tower],
            send_sem=comp_send.at[off],
            recv_sem=comp_recv.at[off],
            device_id={"tower": lax.rem(tower + off, towers)},
            device_id_type=MESH,
        )
        copy.start()
        shares.append(copy)
    for copy in shares:
        copy.wait()

    tail = jnp.concatenate([squeezed[t] for t in range(towers)], axis=1)
    mixes = []
    for e in range(experts):
        value = partial[e] + jnp.dot(tail, expert_w[e, other_width:, :], preferred_element_type=jnp.float32)
        value = jnp.maximum(value, 0.0).astype(jnp.bfloat16)
        for t in range(towers):
            hidden_out[t, e] = value[:, t * half : (t + 1) * half]
        for off in range(1, towers):
            peer = lax.rem(tower + off, towers)
            copy = pltpu.make_async_remote_copy(
                src_ref=hidden_out.at[peer, e],
                dst_ref=hidden_in.at[tower, e],
                send_sem=hid_send.at[off, e],
                recv_sem=hid_recv.at[off, e],
                device_id={"tower": peer},
                device_id_type=MESH,
            )
            copy.start()
            mixes.append(copy)
        hidden_in[tower, e] = hidden_out[tower, e]
    logits = logits + lax.dot_general(tail, gate_ref[:, other_width:], nt, preferred_element_type=jnp.float32)
    weights = jnp.exp(logits)
    count = experts * towers
    gates = []
    for k in range(tasks):
        mine = weights[:, k * count : (k + 1) * count]
        gates.append(mine / jnp.sum(mine, axis=1, keepdims=True))
    for copy in mixes:
        copy.wait()
    for r in range(0, rows, 32):
        sums = [jnp.zeros((32, half), jnp.float32) for _ in range(tasks)]
        for t in range(towers):
            for e in range(experts):
                value = hidden_in[t, e, r : r + 32, :].astype(jnp.float32)
                m = t * experts + e
                sums = [sums[k] + gates[k][r : r + 32, m : m + 1] * value for k in range(tasks)]
        for k in range(tasks):
            out_ref[r : r + 32, k * half : (k + 1) * half] = sums[k].astype(out_ref.dtype)


def dense(inverse, sendable, cross_w, cross_b, comp_w, comp_b, other, expert_w, expert_b, gate):
    inner, share, rows = sendable.shape
    towers = lax.axis_size("tower")
    total = cross_w.shape[0]
    experts, _, hid = expert_w.shape
    tasks = gate.shape[0] // (experts * towers)
    half = hid // towers
    low, full = jnp.bfloat16, jnp.float32
    vmem = pl.BlockSpec(memory_space=pltpu.VMEM)
    smem = pl.BlockSpec(memory_space=pltpu.SMEM)
    dma = pltpu.SemaphoreType.DMA
    return pl.pallas_call(
        dense_kernel,
        out_shape=jax.ShapeDtypeStruct((rows, tasks * half), low),
        in_specs=[smem] + [vmem] * 6 + [pl.BlockSpec(memory_space=pltpu.HBM)] + [vmem] * 2,
        out_specs=vmem,
        scratch_shapes=[
            pltpu.VMEM((inner, share, rows), low),
            pltpu.VMEM((inverse.shape[0], total // inverse.shape[0], rows), full),
            pltpu.VMEM((total, rows), full),
            pltpu.VMEM((rows, total), full),
            pltpu.VMEM(expert_w.shape, low),
            pltpu.VMEM((experts, rows, hid), full),
            pltpu.VMEM((towers, rows, comp_w.shape[0]), low),
            pltpu.VMEM((towers, experts, rows, half), low),
            pltpu.VMEM((towers, experts, rows, half), low),
            dma,
            dma,
            dma((inner,)),
            dma((inner,)),
            dma((towers,)),
            dma((towers,)),
            dma((towers, experts)),
            dma((towers, experts)),
        ],
        compiler_params=pltpu.CompilerParams(collective_id=0, has_side_effects=True, vmem_limit_bytes=24 * 2**20),
    )(inverse, sendable, cross_w, cross_b, comp_w, comp_b, other, expert_w, expert_b, gate)


def on_device(
    ids, bag_len, slot_of_feature, tables, cross_w, cross_b, comp_w, comp_b, other_towers, expert_w, expert_b, gate_w
):
    sendable = pool(tables[0], ids[0], bag_len[0], lax.axis_size("inner"))
    slots = jnp.arange(slot_of_feature.shape[1], dtype=jnp.int32)
    inverse = jnp.sum(jnp.where(slot_of_feature[0][:, None] == slots[None, :], slots[:, None], 0), axis=0)
    ein, tasks, experts = gate_w.shape
    gate = jnp.transpose(gate_w, (1, 2, 0)).reshape(tasks * experts, ein)
    mixed = dense(
        inverse, sendable, cross_w[0], cross_b, jnp.transpose(comp_w[0]), comp_b, other_towers, expert_w, expert_b, gate
    )
    return mixed.reshape(mixed.shape[0], tasks, -1)


def solution(mesh):
    return jax.shard_map(
        on_device,
        mesh=mesh,
        in_specs=(
            P("tower", "inner", "groups", None),
            P("tower", "inner", "groups"),
            P("tower", None),
            P("tower", "inner", None, None),
            P("tower", None, None),
            P("tower", None),
            P("tower", None, None),
            P("tower", None),
            P(("groups", "inner"), None),
            P("tower", None, None),
            P("tower", None),
            P(),
        ),
        out_specs=P(("groups", "inner"), None, "tower"),
        check_vma=False,
    )
```

time: 635 us -> 87.2 us (0.14)
  local copies, waits for them, and re-layouts: 549 us -> 3.1 us
  Pallas kernels: 0 us -> 81 us
  other arithmetic: 49.6 us -> 2.43 us
  waiting for transfers between devices: 10.2 us -> 0 us
  starting transfers between devices: 9.35 us -> 0 us
  matrix products: 6.7 us -> 0 us
    gather x1 -> x0, local copies, waits for them, and re-layouts: 501 us -> none  [pool_features(): gathered = jnp.take(flat_table, flat_ids, axis=0, mode='clip')]
    pallas_call x0 -> x2, Pallas kernels: none -> 81 us  [the longest x1 62.2 us: pool(): pl.pallas_call(functools.partial(pool_kernel, bag, unroll), out_shape=jax...]
    unnamed x3 -> x1, other arithmetic: 47 us -> 1.54 us
    unnamed x22 -> x17, local copies, waits for them, and re-layouts: 29.8 us -> 2.22 us
    all_to_all x1 -> x0, waiting for transfers between devices: 10.2 us -> none  [on_device(): lax.all_to_all(sendable, 'inner', split_axis=0, concat_axis=3, tiled=True)]
    all_to_all x1 -> x0, starting transfers between devices: 9.35 us -> none  [on_device(): lax.all_to_all(sendable, 'inner', split_axis=0, concat_axis=3, tiled=True)]
    add x2 -> x0, local copies, waits for them, and re-layouts: 8.48 us -> none  [pool_features(): indices + offsets]
    dot_general x3 -> x0, matrix products: 6.49 us -> none  [the longest x1 3.34 us: on_device(): jnp.dot(next_layer, comp_w[0], preferred_element_type=jnp.float32)]
  transfers between devices with their start and end apart: 1 -> 0, of which waited for: 1 -> 0; matrix products, arithmetic and copies ran while one was open for 0% -> 0% of each run, Pallas kernels for 0% -> 0%
where the time goes in v1:
time: 87.2 us; the launch traced here: 86.7 us
  Pallas kernels  81 us (93%)
  local copies, waits for them, and re-layouts  3.1 us (4%)
  other arithmetic  2.43 us (3%)
    pallas_call x1, Pallas kernels, pool(): pl.pallas_call(functools.partial(pool_kernel, bag, unroll), out_shape=jax...  62.2 us
    pallas_call x1, Pallas kernels, dense(): pl.pallas_call(dense_kernel, out_shape=jax.ShapeDtypeStruct((rows, tasks...  18.8 us
    unnamed x17, local copies, waits for them, and re-layouts  2.22 us

profile of v1, /device:TPU:0, one launch (start us, length us, event | category | flops | bytes accessed | tf_op | source)
XLA Modules:
  0.0 86.7 jit_solution(12257139038545973550)
XLA Ops:
  0.0 0.0 copy-start.4
  0.0 0.0 copy-start.5
  0.0 0.0 copy-start.2
  0.0 0.0 copy-start.7
  0.0 0.0 copy-start.3
  0.0 0.0 copy-start.6
  0.0 0.0 copy-start
  0.0 0.9 %select_reduce_fusion.inverse_ref = s32[64]{0:T(128)S(1)} fusion(s32[64]{0:T(128)} %bitcast.27), kind=kLoop, calls=%fused_computation.3 | loop fusion | flops 12224 | bytes 512 | tf_op jit(solution)/shard_map/reduce_sum | solution.py:247
  0.9 1.5 %fusion = s32[8,8,4,128]{3,2,1,0:T(4,128)S(1)} fusion(s32[1,8,1024,4]{2,3,1,0:T(4,128)} %param.12, s32[8,1024]{1,0:T(8,128)} %bitcast.26), kind=kLoop, calls=%fused_computation.1 | loop fusion | flops 65536 | bytes 294912
  2.5 62.2 %shard_map.118.send_ref = bf16[8,192,128]{2,1,0:T(8,128)(2,1)S(1)} custom-call(s32[32768]{0:T(1024)S(1)} %bitcast.22, bf16[8,24,16384]{2,1,0:T(8,128)(2,1)} %bitcast.25), custom_call_target="tpu_custom_call" | custom-call | tf_op jit(solution)/shard_map/pallas_call | solution.py:59
  64.7 0.0 copy-done.4
  64.7 0.0 copy-done.5
  64.8 0.0 copy-done.2
  64.8 0.0 copy-done.7
  64.8 0.0 copy-done.3
  64.8 0.0 copy-done.6
  64.8 0.0 copy-done
  64.8 0.0 copy-start.1
  64.8 2.2 %copy-done.1 = bf16[4,1024,512]{2,1,0:T(8,128)(2,1)S(1)} copy-done((bf16[4,1024,512]{2,1,0:T(8,128)(2,1)S(1)}, bf16[4,1024,512]{2,1,0:T(8,128)(2,1)}, u32[]{:S(2)}) %copy-start.1) | copy-done | bytes 4194328
  67.0 18.8 %shard_map.119 = bf16[128,1024]{1,0:T(8,128)(2,1)S(1)} custom-call(s32[64]{0:T(128)S(1)} %select_reduce_fusion.inverse_ref, bf16[8,192,128]{2,1,0:T(8,128)(2,1)S(1)} %shard_map.118.send_ref, bf16[1536,1536]{1,0:T(8,128)(2,1)S(1)} %bitcast.21, f32[1,1536]{1,0:T(1,128)S(1)} %copy-done.6, bf16[64,1536]{1,0:T(8,128)(2,1)S(1)} %bitcast.23, ...), custom_call_target="tpu_custom_call" | custom-call | tf_op jit(solution)/shard_map/pallas_call | solution.py:214
  85.8 0.9 %reshape.13 = bf16[128,4,256]{2,1,0:T(4,128)(2,1)} reshape(bf16[128,1024]{1,0:T(8,128)(2,1)S(1)} %shard_map.119) | data formatting | bytes 524288 | tf_op jit(solution)/shard_map/reshape | solution.py:253
  (1 shorter events, 0.0 us)
Async XLA Ops:
  0.0 64.7 %copy-start.4 = (bf16[1024,4,8]{0,2,1:T(8,128)(2,1)S(1)}, bf16[1024,4,8]{0,2,1:T(8,128)(2,1)}, u32[]{:S(2)}) copy-start(bf16[1024,4,8]{0,2,1:T(8,128)(2,1)} %param.23) | copy-start | bytes 196612
  0.0 64.7 %copy-start.5 = (f32[4,512]{1,0:T(4,128)S(1)}, f32[4,512]{1,0:T(4,128)}, u32[]{:S(2)}) copy-start(f32[4,512]{1,0:T(4,128)} %expert_b_ref.1) | copy-start | bytes 24580
  0.0 64.8 %copy-start.2 = (bf16[128,896]{1,0:T(8,128)(2,1)S(1)}, bf16[128,896]{1,0:T(8,128)(2,1)}, u32[]{:S(2)}) copy-start(bf16[128,896]{1,0:T(8,128)(2,1)} %other_ref.1) | copy-start | bytes 688132
  0.0 64.8 %copy-start.7 = (f32[1,64]{1,0:T(1,128)S(1)}, f32[1,64]{1,0:T(1,128)}, u32[]{:S(2)}) copy-start(f32[1,64]{1,0:T(1,128)} %comp_b_ref.1) | copy-start | bytes 772
  0.0 64.8 %copy-start.3 = (bf16[1,1536,64]{1,2,0:T(8,128)(2,1)S(1)}, bf16[1,1536,64]{1,2,0:T(8,128)(2,1)}, u32[]{:S(2)}) copy-start(bf16[1,1536,64]{1,2,0:T(8,128)(2,1)} %param.18) | copy-start | bytes 589828
  0.0 64.8 %copy-start.6 = (f32[1,1536]{1,0:T(1,128)S(1)}, f32[1,1536]{1,0:T(1,128)}, u32[]{:S(2)}) copy-start(f32[1,1536]{1,0:T(1,128)} %cross_b_ref.1) | copy-start | bytes 18436
  0.0 64.8 %copy-start = (bf16[1,1536,1536]{2,1,0:T(8,128)(2,1)S(1)}, bf16[1,1536,1536]{2,1,0:T(8,128)(2,1)}, u32[]{:S(2)}) copy-start(bf16[1,1536,1536]{2,1,0:T(8,128)(2,1)} %param.16) | copy-start | bytes 14155780
  64.8 2.2 %copy-start.1 = (bf16[4,1024,512]{2,1,0:T(8,128)(2,1)S(1)}, bf16[4,1024,512]{2,1,0:T(8,128)(2,1)}, u32[]{:S(2)}) copy-start(bf16[4,1024,512]{2,1,0:T(8,128)(2,1)} %expert_w_hbm.1) | copy-start | bytes 12582916

commit v2 on v1

--- a/solution.py
+++ b/solution.py
@@ -9,66 +9,85 @@
 MESH = pl.DeviceIdType.MESH
 
 
-def pool_kernel(bag, unroll, ids_ref, tab_ref, out_ref, rows_ref, acc_ref):
-    group, width, vocab = tab_ref.shape
+def pool_kernel(bag, ids_ref, tab_hbm, out_ref, tab_ref, rows_a, rows_b, acc_ref, sem):
+    features, width, vocab = tab_ref.shape
     dests, _, block = out_ref.shape
     samples = dests * block
-    lanes = rows_ref.shape[1]
-    first = pl.program_id(0) * (group * bag * samples)
-
-    def turn(c, carry):
+    lanes = acc_ref.shape[1]
+    group = max(g for g in range(1, features + 1) if features % g == 0 and g * width <= lanes)
+    steps = vocab // lanes
+    each = samples // steps
+    rows = (rows_a, rows_b)
+    lane = lax.broadcasted_iota(jnp.int32, (1, lanes), 1)
+    inside = [lane < (f + 1) * width for f in range(group)]
+    loads = []
+    for i in range(features // group):
+        part = pl.ds(i * group, group)
+        loads.append(pltpu.make_async_copy(tab_hbm.at[part], tab_ref.at[part], sem.at[i]))
+        loads[-1].start()
+
+    def turn(i, c):
         at = pl.multiple_of(c * lanes, lanes)
-        parts = [tab_ref[f, :, pl.ds(at, lanes)].astype(jnp.float32) for f in range(group)]
+        parts = [tab_ref[i * group + f, :, pl.ds(at, lanes)].astype(jnp.float32) for f in range(group)]
         if lanes > group * width:
             parts.append(jnp.zeros((lanes - group * width, lanes), jnp.float32))
-        rows_ref[pl.ds(at, lanes), :] = jnp.concatenate(parts, axis=0).T
-        return carry
-
-    lax.fori_loop(0, vocab // lanes, turn, 0)
-    rows_ref[pl.ds(vocab, 8), :] = jnp.zeros((8, lanes), jnp.float32)
-    lane = lax.broadcasted_iota(jnp.int32, (1, lanes), 1)
-    inside = [lane < (f + 1) * width for f in range(group)]
-
-    def look(n, carry):
-        base = n * unroll
-        for u in range(unroll):
+        rows[i % 2][pl.ds(at, lanes), :] = jnp.concatenate(parts, axis=0).T
+
+    def look(i, c):
+        base = c * each
+        held = rows[i % 2]
+        for u in range(each):
             total = None
             for f in reversed(range(group)):
-                got = [
-                    rows_ref[pl.ds(ids_ref[first + (f * bag + j) * samples + base + u], 1), :]
-                    for j in range(bag)
-                ]
+                got = []
+                for j in range(bag):
+                    at = ((i * group + f) * bag + j) * samples + u
+                    got.append(held[pl.ds(ids_ref.at[pl.ds(at, samples)][base], 1), :])
                 while len(got) > 1:
                     got = [a + b for a, b in zip(got[::2], got[1::2])] + got[len(got) & ~1 :]
                 total = got[0] if total is None else jnp.where(inside[f], got[0], total)
             acc_ref[pl.ds(base + u, 1), :] = total
-        return carry
-
-    lax.fori_loop(0, samples // unroll, look, 0)
-    for d in range(dests):
-        turned = acc_ref[pl.ds(d * block, block), :].T
-        out_ref[d] = turned[: group * width].astype(out_ref.dtype)
-
-
-def pool(tables, ids, lengths, dests, unroll=16):
+
+    for held in rows:
+        held[pl.ds(vocab, 8), :] = jnp.zeros((8, lanes), jnp.float32)
+    count = features // group
+    for phase in range(count + 1):
+        if phase < count:
+            loads[phase].wait()
+
+        def body(c, carry):
+            if phase < count:
+                turn(phase, c)
+            if phase > 0:
+                look(phase - 1, c)
+            return carry
+
+        lax.fori_loop(0, steps, body, 0)
+        if phase > 0:
+            first = (phase - 1) * group * width
+            for d in range(dests):
+                turned = acc_ref[pl.ds(d * block, block), :].T
+                out_ref[d, first : first + group * width, :] = turned[: group * width].astype(out_ref.dtype)
+
+
+def pool(tables, ids, lengths, dests):
     features, vocab, width = tables.shape
     samples, bag = ids.shape[1:]
-    group = max(g for g in range(1, features + 1) if features % g == 0 and g * width <= 128)
     in_bag = jnp.arange(bag)[None, :, None] < lengths[:, None, :]
     flat = jnp.where(in_bag, jnp.transpose(ids, (0, 2, 1)), vocab).reshape(-1)
+    flat = jnp.pad(flat, (0, 1024))
     return pl.pallas_call(
-        functools.partial(pool_kernel, bag, unroll),
+        functools.partial(pool_kernel, bag),
         out_shape=jax.ShapeDtypeStruct((dests, features * width, samples // dests), jnp.bfloat16),
-        grid_spec=pltpu.PrefetchScalarGridSpec(
-            num_scalar_prefetch=1,
-            grid=(features // group,),
-            in_specs=[pl.BlockSpec((group, width, vocab), lambda i, ids: (i, 0, 0))],
-            out_specs=pl.BlockSpec((dests, group * width, samples // dests), lambda i, ids: (0, i, 0)),
-            scratch_shapes=[
-                pltpu.VMEM((vocab + 8, 128), jnp.float32),
-                pltpu.VMEM((samples, 128), jnp.float32),
-            ],
-        ),
+        in_specs=[pl.BlockSpec(memory_space=pltpu.SMEM), pl.BlockSpec(memory_space=pltpu.HBM)],
+        out_specs=pl.BlockSpec(memory_space=pltpu.VMEM),
+        scratch_shapes=[
+            pltpu.VMEM((features, width, vocab), jnp.bfloat16),
+            pltpu.VMEM((vocab + 8, 128), jnp.float32),
+            pltpu.VMEM((vocab + 8, 128), jnp.float32),
+            pltpu.VMEM((samples, 128), jnp.float32),
+            pltpu.SemaphoreType.DMA((features,)),
+        ],
         compiler_params=pltpu.CompilerParams(vmem_limit_bytes=48 * 2**20),
     )(flat, jnp.transpose(tables, (0, 2, 1)))
 

time: 87.2 us -> 65.8 us (0.75)
  Pallas kernels: 81 us -> 59.6 us
    pallas_call x1, Pallas kernels: 62.2 us -> 40.8 us  [pool(): pl.pallas_call(functools.partial(pool_kernel, bag), out_shape=jax.ShapeDt...]
where the time goes in v2:
time: 65.8 us; the launch traced here: 65.3 us
  Pallas kernels  59.6 us (91%)
  local copies, waits for them, and re-layouts  3.11 us (5%)
  other arithmetic  2.43 us (4%)
    pallas_call x1, Pallas kernels, pool(): pl.pallas_call(functools.partial(pool_kernel, bag), out_shape=jax.ShapeDt...  40.8 us
    pallas_call x1, Pallas kernels, dense(): pl.pallas_call(dense_kernel, out_shape=jax.ShapeDtypeStruct((rows, tasks...  18.8 us
    unnamed x17, local copies, waits for them, and re-layouts  2.22 us
    unnamed x1, other arithmetic  1.54 us

profile of v2, /device:TPU:0, one launch (start us, length us, event | category | flops | bytes accessed | tf_op | source)
XLA Modules:
  0.0 65.3 jit_solution(17457207976186637901)
XLA Ops:
  0.0 0.0 copy-start.4
  0.0 0.0 copy-start.5
  0.0 0.0 copy-start.2
  0.0 0.0 copy-start.7
  0.0 0.0 copy-start.3
  0.0 0.0 copy-start.6
  0.0 0.0 copy-start
  0.0 0.9 %select_reduce_fusion.inverse_ref = s32[64]{0:T(128)S(1)} fusion(s32[64]{0:T(128)} %bitcast.27), kind=kLoop, calls=%fused_computation.3 | loop fusion | flops 12224 | bytes 512 | tf_op jit(solution)/shard_map/reduce_sum | solution.py:266
  0.9 1.5 %fusion = s32[8,8,4,128]{3,2,1,0:T(4,128)S(1)} fusion(s32[1,8,1024,4]{2,3,1,0:T(4,128)} %param.12, s32[8,1024]{1,0:T(8,128)} %bitcast.26), kind=kLoop, calls=%fused_computation.1 | loop fusion | flops 65536 | bytes 294912
  2.5 40.8 %shard_map.118.send_ref = bf16[8,192,128]{2,1,0:T(8,128)(2,1)S(1)} custom-call(s32[33792]{0:T(1024)S(1)} %pad.4.ids_ref, bf16[8,24,16384]{2,1,0:T(8,128)(2,1)} %bitcast.24), custom_call_target="tpu_custom_call" | custom-call | tf_op jit(solution)/shard_map/pallas_call | solution.py:79
  43.3 0.0 copy-done.4
  43.3 0.0 copy-done.5
  43.3 0.0 copy-done.2
  43.3 0.0 copy-done.7
  43.3 0.0 copy-done.3
  43.4 0.0 copy-done.6
  43.4 0.0 copy-done
  43.4 0.0 copy-start.1
  43.4 2.2 %copy-done.1 = bf16[4,1024,512]{2,1,0:T(8,128)(2,1)S(1)} copy-done((bf16[4,1024,512]{2,1,0:T(8,128)(2,1)S(1)}, bf16[4,1024,512]{2,1,0:T(8,128)(2,1)}, u32[]{:S(2)}) %copy-start.1) | copy-done | bytes 4194328
  45.6 18.8 %shard_map.119 = bf16[128,1024]{1,0:T(8,128)(2,1)S(1)} custom-call(s32[64]{0:T(128)S(1)} %select_reduce_fusion.inverse_ref, bf16[8,192,128]{2,1,0:T(8,128)(2,1)S(1)} %shard_map.118.send_ref, bf16[1536,1536]{1,0:T(8,128)(2,1)S(1)} %bitcast.21, f32[1,1536]{1,0:T(1,128)S(1)} %copy-done.6, bf16[64,1536]{1,0:T(8,128)(2,1)S(1)} %bitcast.22, ...), custom_call_target="tpu_custom_call" | custom-call | tf_op jit(solution)/shard_map/pallas_call | solution.py:233
  64.4 0.9 %reshape.13 = bf16[128,4,256]{2,1,0:T(4,128)(2,1)} reshape(bf16[128,1024]{1,0:T(8,128)(2,1)S(1)} %shard_map.119) | data formatting | bytes 524288 | tf_op jit(solution)/shard_map/reshape | solution.py:272
  (2 shorter events, 0.0 us)
Async XLA Ops:
  0.0 43.3 %copy-start.4 = (bf16[1024,4,8]{0,2,1:T(8,128)(2,1)S(1)}, bf16[1024,4,8]{0,2,1:T(8,128)(2,1)}, u32[]{:S(2)}) copy-start(bf16[1024,4,8]{0,2,1:T(8,128)(2,1)} %param.23) | copy-start | bytes 196612
  0.0 43.3 %copy-start.5 = (f32[4,512]{1,0:T(4,128)S(1)}, f32[4,512]{1,0:T(4,128)}, u32[]{:S(2)}) copy-start(f32[4,512]{1,0:T(4,128)} %expert_b_ref.1) | copy-start | bytes 24580
  0.0 43.3 %copy-start.2 = (bf16[128,896]{1,0:T(8,128)(2,1)S(1)}, bf16[128,896]{1,0:T(8,128)(2,1)}, u32[]{:S(2)}) copy-start(bf16[128,896]{1,0:T(8,128)(2,1)} %other_ref.1) | copy-start | bytes 688132
  0.0 43.3 %copy-start.7 = (f32[1,64]{1,0:T(1,128)S(1)}, f32[1,64]{1,0:T(1,128)}, u32[]{:S(2)}) copy-start(f32[1,64]{1,0:T(1,128)} %comp_b_ref.1) | copy-start | bytes 772
  0.0 43.3 %copy-start.3 = (bf16[1,1536,64]{1,2,0:T(8,128)(2,1)S(1)}, bf16[1,1536,64]{1,2,0:T(8,128)(2,1)}, u32[]{:S(2)}) copy-start(bf16[1,1536,64]{1,2,0:T(8,128)(2,1)} %param.18) | copy-start | bytes 589828
  0.0 43.3 %copy-start.6 = (f32[1,1536]{1,0:T(1,128)S(1)}, f32[1,1536]{1,0:T(1,128)}, u32[]{:S(2)}) copy-start(f32[1,1536]{1,0:T(1,128)} %cross_b_ref.1) | copy-start | bytes 18436
  0.0 43.3 %copy-start = (bf16[1,1536,1536]{2,1,0:T(8,128)(2,1)S(1)}, bf16[1,1536,1536]{2,1,0:T(8,128)(2,1)}, u32[]{:S(2)}) copy-start(bf16[1,1536,1536]{2,1,0:T(8,128)(2,1)} %param.16) | copy-start | bytes 14155780
  43.4 2.2 %copy-start.1 = (bf16[4,1024,512]{2,1,0:T(8,128)(2,1)S(1)}, bf16[4,1024,512]{2,1,0:T(8,128)(2,1)}, u32[]{:S(2)}) copy-start(bf16[4,1024,512]{2,1,0:T(8,128)(2,1)} %expert_w_hbm.1) | copy-start | bytes 12582916
